TPU v7x, 32 devices: a whole 2x2x4 slice. The times are simulated.
32 devices in a mesh: rep: 2 (over y), fsdp: 4 (over z), section: 4 (over x, core).
Axes of the slice: x: 2, y: 2, z: 4, core: 2. Of those that a mesh axis runs over, the one named last changes fastest.
Arguments:
- iterate: bfloat16 [8, 3072, 1024], P(('rep', 'section'), None, 'fsdp'), parts along dimension 0, may hold values from -0.1875 to 0.1875
Outputs:
- update: bfloat16 [8, 3072, 1024], P(('rep', 'section'), None, 'fsdp'), parts along dimension 0
There are 2 independent parts, one for each index of `rep`. A program takes and returns all parts, laid end to end along the dimension named above; each array names one. Nothing has to cross between parts.
All inputs are finite; a program needn't handle non-finite values.
Results may differ from a plain program's by a relative error of at most 0.0055.
Values may be sent and summed in bfloat16 or wider, within the bound.
A program may use at most 128 MiB of HBM per device.

v0:
```python
import functools
import math

import jax
import jax.numpy as jnp
import numpy as np
from jax import lax
from jax.experimental import pallas as pl
from jax.experimental.pallas import tpu as pltpu
from jax.sharding import PartitionSpec as P


def tile_table(devices, band_blocks):
    block_table = np.zeros((devices, devices), dtype=np.int32)
    for row_block in range(devices):
        for col_block in range(devices):
            distance = (col_block - row_block) % devices
            if distance <= devices // 2:
                block_table[row_block, col_block] = row_block * band_blocks + distance
            else:
                block_table[row_block, col_block] = (
                    devices * band_blocks + col_block * band_blocks + (devices - distance)
                )
    return block_table


def on_device(iterate):
    devices = lax.axis_size("fsdp")
    experts, rows_all, columns = iterate.shape
    strip_rows = rows_all // devices
    band_blocks = devices // 2 + 1
    out_scale = 0.2 * math.sqrt(max(rows_all, columns * devices))
    expert_rows = iterate[0]
    row_blocks = expert_rows.reshape(devices, strip_rows, columns)

    def one_offset(offset):
        partner = jnp.roll(row_blocks, -offset, axis=0)
        tiles = jnp.einsum("nsc,ntc->nst", row_blocks, partner, preferred_element_type=jnp.float32)
        return tiles.astype(jnp.bfloat16)

    band_term = lax.map(one_offset, jnp.arange(band_blocks, dtype=jnp.int32))
    received = lax.all_to_all(band_term, "fsdp", split_axis=1, concat_axis=1, tiled=True)
    own_band = jnp.sum(received.astype(jnp.float32), axis=1).astype(jnp.bfloat16)
    upper_tiles = lax.all_gather(own_band, "fsdp", axis=0, tiled=True)
    tile_pool = jnp.concatenate([upper_tiles, jnp.swapaxes(upper_tiles, 1, 2)], axis=0)
    block_table = jnp.asarray(tile_table(devices, band_blocks))
    dense_blocks = jnp.take(tile_pool, block_table, axis=0)

    def apply_gram(operand):
        shaped = operand.reshape(devices, strip_rows, columns)
        product = jnp.einsum(
            "nmij,mjc->nic", dense_blocks, shaped, preferred_element_type=jnp.float32
        )
        return product.reshape(rows_all, columns)

    first_product = apply_gram(expert_rows)
    second_product = apply_gram(first_product.astype(jnp.bfloat16))
    combined = out_scale * (
        3.4445 * expert_rows.astype(jnp.float32) - 4.775 * first_product + 2.0315 * second_product
    )
    results = [combined.astype(jnp.bfloat16)]
    return jnp.stack(results)


CHUNK = 128
GROUP = 2
EXTRA = 0
SHIFT = 4.775 / (2 * 2.0315)
BASE = 3.4445 - 4.775 * 4.775 / (4 * 2.0315)


def line_kernel(
    out_scale, chunks, direct,
    x_ref, out_ref,
    xall, gram, half, mixing, staged, sent_rows,
    local_sem, store_sem, recv_sem, inner_sem, outer_sem, mix_send, mix_recv, row_send, row_recv,
):
    me = lax.axis_index("fsdp")
    columns = x_ref.shape[1]
    width = columns * 4
    span = CHUNK * GROUP
    middle = jnp.logical_and(me > 0, me < 3)
    end = jnp.logical_not(middle)

    def rows_of(k):
        return pl.ds(pl.multiple_of(k * CHUNK, CHUNK), CHUNK)

    own_copy = pltpu.make_async_copy(x_ref, xall.at[me], local_sem)
    own_copy.start()

    barrier = pltpu.get_barrier_semaphore()

    @pl.when(me > 0)
    def _():
        pl.semaphore_signal(barrier, inc=1, device_id={"fsdp": me - 1}, device_id_type=pl.DeviceIdType.MESH)

    @pl.when(me < 3)
    def _():
        pl.semaphore_signal(barrier, inc=1, device_id={"fsdp": me + 1}, device_id_type=pl.DeviceIdType.MESH)

    @pl.when(middle)
    def _():
        pl.semaphore_wait(barrier, 2)

    @pl.when(end)
    def _():
        pl.semaphore_wait(barrier, 1)

    def own_chunk(k, sem, target):
        return pltpu.make_async_remote_copy(
            src_ref=x_ref.at[rows_of(k)], dst_ref=xall.at[me, rows_of(k)],
            send_sem=sem, recv_sem=recv_sem.at[me, k],
            device_id={"fsdp": target}, device_id_type=pl.DeviceIdType.MESH,
        )

    def relay_chunk(shard, k, sem, target):
        return pltpu.make_async_remote_copy(
            src_ref=xall.at[shard, rows_of(k)], dst_ref=xall.at[shard, rows_of(k)],
            send_sem=sem, recv_sem=recv_sem.at[shard, k],
            device_id={"fsdp": target}, device_id_type=pl.DeviceIdType.MESH,
        )

    def mix_copy(target):
        return pltpu.make_async_remote_copy(
            src_ref=mixing.at[0], dst_ref=mixing.at[0],
            send_sem=mix_send, recv_sem=mix_recv,
            device_id={"fsdp": target}, device_id_type=pl.DeviceIdType.MESH,
        )

    def row_copy(k, target):
        return pltpu.make_async_remote_copy(
            src_ref=sent_rows.at[pl.ds(pl.multiple_of((k - direct) * CHUNK, CHUNK), CHUNK)],
            dst_ref=out_ref.at[rows_of(k)],
            send_sem=row_send.at[k], recv_sem=row_recv.at[k],
            device_id={"fsdp": target}, device_id_type=pl.DeviceIdType.MESH,
        )

    def wide(rows):
        return jnp.concatenate([xall[q, rows, :] for q in range(4)], axis=1)

    def update_rows(shard, slot, rows):
        product = jnp.dot(wide(rows), mixing[slot], preferred_element_type=jnp.float32)
        own = xall[shard, rows, :].astype(jnp.float32)
        return (out_scale * BASE * own + product).astype(jnp.bfloat16)

    def store_copy(k):
        return pltpu.make_async_copy(staged.at[rows_of(k)], out_ref.at[rows_of(k)], store_sem.at[k])

    @pl.when(middle)
    def _():
        peer = 3 - me
        outer = 3 * (me - 1)
        far = 3 - outer

        @pl.loop(0, chunks)
        def _(k):
            own_chunk(k, inner_sem.at[0, k], peer).start()

            @pl.when(k < direct)
            def _():
                own_chunk(k, outer_sem.at[0, k], outer).start()

        for i in range(4):
            row_ids = lax.broadcasted_iota(jnp.int32, (columns, width), 0) + i * columns
            column_ids = lax.broadcasted_iota(jnp.int32, (columns, width), 1)
            gram[i] = jnp.where(row_ids == column_ids, jnp.float32(-SHIFT), jnp.float32(0))
        own_copy.wait()

        @pl.loop(0, chunks)
        def _(k):
            relay_chunk(outer, k, inner_sem.at[1, k], peer).wait_recv()
            relay_chunk(outer, k, inner_sem.at[1, k], peer).start()
            relay_chunk(peer, k, outer_sem.at[1, k], outer).wait_recv()

            @pl.when(k < direct)
            def _():
                relay_chunk(peer, k, outer_sem.at[1, k], outer).start()

        def take_far(k):
            relay_chunk(far, k, outer_sem.at[2, k], outer).wait_recv()

            @pl.when(k < direct)
            def _():
                relay_chunk(far, k, outer_sem.at[2, k], outer).start()

        def partial(step, i):
            rows = pl.ds(pl.multiple_of(step * span, span), span)
            return lax.dot_general(
                xall[i, rows, :], wide(rows), (((0,), (0,)), ((), ())),
                preferred_element_type=jnp.float32,
            )

        steps = chunks // GROUP

        @pl.loop(0, steps - 1)
        def _(step):
            for g in range(GROUP):
                take_far(step * GROUP + g)
            for i in range(4):
                gram[i] += partial(step, i)

        for g in range(GROUP):
            take_far((steps - 1) * GROUP + g)
        for i in range(4):
            total = (gram[i] + partial(steps - 1, i)).astype(jnp.bfloat16)
            for j in range(4):
                half[j, i * columns:(i + 1) * columns, :] = total[:, j * columns:(j + 1) * columns]

        def mix(slot, shard):
            for i in range(4):
                left = jnp.concatenate(
                    [half[j, i * columns:(i + 1) * columns, :] for j in range(4)], axis=1
                )
                square = jnp.dot(left, half[shard], preferred_element_type=jnp.float32)
                mixing[slot, i * columns:(i + 1) * columns, :] = (
                    (out_scale * 2.0315) * square
                ).astype(jnp.bfloat16)

        mix(0, outer)
        mix_copy(outer).start()

        @pl.loop(direct, chunks)
        def _(k):
            sent_rows[pl.ds(pl.multiple_of((k - direct) * CHUNK, CHUNK), CHUNK), :] = update_rows(
                outer, 0, rows_of(k)
            )
            row_copy(k, outer).start()

        mix(1, me)

        @pl.loop(0, chunks)
        def _(k):
            staged[rows_of(k), :] = update_rows(me, 1, rows_of(k))
            store_copy(k).start()

        @pl.loop(0, chunks)
        def _(k):
            store_copy(k).wait()
            own_chunk(k, inner_sem.at[0, k], peer).wait_send()
            relay_chunk(outer, k, inner_sem.at[1, k], peer).wait_send()

        @pl.loop(0, direct)
        def _(k):
            own_chunk(k, outer_sem.at[0, k], outer).wait_send()
            relay_chunk(peer, k, outer_sem.at[1, k], outer).wait_send()
            relay_chunk(far, k, outer_sem.at[2, k], outer).wait_send()

        mix_copy(outer).wait_send()

        @pl.loop(direct, chunks)
        def _(k):
            row_copy(k, outer).wait_send()

    @pl.when(end)
    def _():
        inner = 1 + me // 3

        @pl.loop(0, chunks)
        def _(k):
            own_chunk(k, inner_sem.at[0, k], inner).start()

        own_copy.wait()
        for hop in range(3):
            shard = inner + hop * (1 - 2 * (me // 3))

            @pl.loop(0, direct)
            def _(k):
                relay_chunk(shard, k, outer_sem.at[0, k], inner).wait_recv()

        mix_copy(inner).wait_recv()

        @pl.loop(0, direct)
        def _(k):
            staged[rows_of(k), :] = update_rows(me, 0, rows_of(k))
            store_copy(k).start()

        @pl.loop(0, direct)
        def _(k):
            store_copy(k).wait()

        @pl.loop(0, chunks)
        def _(k):
            own_chunk(k, inner_sem.at[0, k], inner).wait_send()

        @pl.loop(direct, chunks)
        def _(k):
            row_copy(k, inner).wait_recv()


def on_device_line(iterate):
    _, rows_all, columns = iterate.shape
    width = columns * 4
    chunks = rows_all // CHUNK
    direct = 2 * chunks // 3 + EXTRA
    out_scale = 0.2 * math.sqrt(max(rows_all, width))
    update = pl.pallas_call(
        functools.partial(line_kernel, out_scale, chunks, direct),
        out_shape=jax.ShapeDtypeStruct((rows_all, columns), jnp.bfloat16),
        in_specs=[pl.BlockSpec(memory_space=pl.ANY)],
        out_specs=pl.BlockSpec(memory_space=pl.ANY),
        scratch_shapes=[
            pltpu.VMEM((4, rows_all, columns), jnp.bfloat16),
            pltpu.VMEM((4, columns, width), jnp.float32),
            pltpu.VMEM((4, width, columns), jnp.bfloat16),
            pltpu.VMEM((2, width, columns), jnp.bfloat16),
            pltpu.VMEM((rows_all, columns), jnp.bfloat16),
            pltpu.VMEM(((chunks - direct) * CHUNK, columns), jnp.bfloat16),
            pltpu.SemaphoreType.DMA,
            pltpu.SemaphoreType.DMA((chunks,)),
            pltpu.SemaphoreType.DMA((4, chunks)),
            pltpu.SemaphoreType.DMA((2, chunks)),
            pltpu.SemaphoreType.DMA((3, chunks)),
            pltpu.SemaphoreType.DMA,
            pltpu.SemaphoreType.DMA,
            pltpu.SemaphoreType.DMA((chunks,)),
            pltpu.SemaphoreType.DMA((chunks,)),
        ],
        compiler_params=pltpu.CompilerParams(
            collective_id=0, has_side_effects=True, vmem_limit_bytes=56 << 20
        ),
    )(iterate[0])
    return update[None]


def for_shapes(iterate):
    _, rows_all, columns = iterate.shape
    devices = lax.axis_size("fsdp")
    fits = columns % 256 == 0 and rows_all % (3 * CHUNK * GROUP) == 0
    if devices == 4 and columns * devices <= rows_all and fits:
        return on_device_line(iterate)
    return on_device(iterate)


def solution(mesh):
    return jax.shard_map(
        for_shapes,
        mesh=mesh,
        in_specs=(P(("rep", "section"), None, "fsdp"),),
        out_specs=P(("rep", "section"), None, "fsdp"),
        check_vma=False,
    )
```

profile of v0, /device:TPU:0, one launch (start us, length us, event | category | flops | bytes accessed | tf_op | source)
XLA Modules:
  0.0 103.2 jit_solution(230794553644554339)
XLA Ops:
  0.0 100.5 %shard_map.17 = bf16[3072,256]{1,0:T(8,128)(2,1)} custom-call(bf16[3072,256]{1,0:T(8,128)(2,1)} %bitcast.3), custom_call_target="tpu_custom_call" | custom-call | tf_op jit(solution)/shard_map/pallas_call | solution.py:296
  100.5 2.7 %copy.3 = bf16[1,3072,256]{2,1,0:T(8,128)(2,1)} copy(bf16[1,3072,256]{2,1,0:T(8,128)(2,1)} %bitcast.2) | data formatting | bytes 3145728
where the time goes:
time: 103 us
  Pallas kernels  101 us (98%)
  local copies, waits for them, and re-layouts  2.65 us (3%)
    pallas_call x1, Pallas kernels, on_device_line(): pl.pallas_call(functools.partial(line_kernel, out_scale, chunks, direct),...  101 us
    unnamed x1, local copies, waits for them, and re-layouts  2.65 us

commit v1 on v0

--- a/solution.py
+++ b/solution.py
@@ -62,9 +62,7 @@
     return jnp.stack(results)
 
 
-CHUNK = 128
-GROUP = 2
-EXTRA = 0
+CHUNK = 256
 SHIFT = 4.775 / (2 * 2.0315)
 BASE = 3.4445 - 4.775 * 4.775 / (4 * 2.0315)
 
@@ -72,13 +70,12 @@
 def line_kernel(
     out_scale, chunks, direct,
     x_ref, out_ref,
-    xall, gram, half, mixing, staged, sent_rows,
-    local_sem, store_sem, recv_sem, inner_sem, outer_sem, mix_send, mix_recv, row_send, row_recv,
+    xall, gram, half, mixing, sent_rows,
+    local_sem, recv_sem, inner_sem, outer_sem, mix_send, mix_recv, row_send, row_recv,
 ):
     me = lax.axis_index("fsdp")
     columns = x_ref.shape[1]
     width = columns * 4
-    span = CHUNK * GROUP
     middle = jnp.logical_and(me > 0, me < 3)
     end = jnp.logical_not(middle)
 
@@ -120,10 +117,11 @@
             device_id={"fsdp": target}, device_id_type=pl.DeviceIdType.MESH,
         )
 
-    def mix_copy(target):
+    def mix_copy(i, target):
+        part = pl.ds(i * columns, columns)
         return pltpu.make_async_remote_copy(
-            src_ref=mixing.at[0], dst_ref=mixing.at[0],
-            send_sem=mix_send, recv_sem=mix_recv,
+            src_ref=mixing.at[0, part], dst_ref=mixing.at[0, part],
+            send_sem=mix_send.at[i], recv_sem=mix_recv.at[i],
             device_id={"fsdp": target}, device_id_type=pl.DeviceIdType.MESH,
         )
 
@@ -143,9 +141,6 @@
         own = xall[shard, rows, :].astype(jnp.float32)
         return (out_scale * BASE * own + product).astype(jnp.bfloat16)
 
-    def store_copy(k):
-        return pltpu.make_async_copy(staged.at[rows_of(k)], out_ref.at[rows_of(k)], store_sem.at[k])
-
     @pl.when(middle)
     def _():
         peer = 3 - me
@@ -163,7 +158,9 @@
         for i in range(4):
             row_ids = lax.broadcasted_iota(jnp.int32, (columns, width), 0) + i * columns
             column_ids = lax.broadcasted_iota(jnp.int32, (columns, width), 1)
-            gram[i] = jnp.where(row_ids == column_ids, jnp.float32(-SHIFT), jnp.float32(0))
+            start = jnp.where(row_ids == column_ids, jnp.float32(-SHIFT), jnp.float32(0))
+            for j in range(4):
+                gram[i, j] = start[:, j * columns:(j + 1) * columns]
         own_copy.wait()
 
         @pl.loop(0, chunks)
@@ -183,30 +180,36 @@
             def _():
                 relay_chunk(far, k, outer_sem.at[2, k], outer).start()
 
-        def partial(step, i):
-            rows = pl.ds(pl.multiple_of(step * span, span), span)
+        def turned(left, right):
             return lax.dot_general(
-                xall[i, rows, :], wide(rows), (((0,), (0,)), ((), ())),
-                preferred_element_type=jnp.float32,
+                left, right, (((0,), (0,)), ((), ())), preferred_element_type=jnp.float32
             )
 
-        steps = chunks // GROUP
-
-        @pl.loop(0, steps - 1)
-        def _(step):
-            for g in range(GROUP):
-                take_far(step * GROUP + g)
+        @pl.loop(0, chunks - 1)
+        def _(k):
+            take_far(k)
             for i in range(4):
-                gram[i] += partial(step, i)
-
-        for g in range(GROUP):
-            take_far((steps - 1) * GROUP + g)
-        for i in range(4):
-            total = (gram[i] + partial(steps - 1, i)).astype(jnp.bfloat16)
-            for j in range(4):
-                half[j, i * columns:(i + 1) * columns, :] = total[:, j * columns:(j + 1) * columns]
-
-        def mix(slot, shard):
+                product = turned(xall[i, rows_of(k), :], wide(rows_of(k)))
+                for j in range(4):
+                    gram[i, j] += product[:, j * columns:(j + 1) * columns]
+
+        last = rows_of(chunks - 1)
+
+        def finish(i, j):
+            total = gram[i, j] + turned(xall[i, last, :], xall[j, last, :])
+            half[j, pl.ds(pl.multiple_of(i * columns, columns), columns), :] = total.astype(jnp.bfloat16)
+
+        near = (me, peer, outer)
+        for i in near:
+            for j in near:
+                finish(i, j)
+        take_far(chunks - 1)
+        for i in near:
+            finish(far, i)
+            finish(i, far)
+        finish(far, far)
+
+        def mix(slot, shard, send):
             for i in range(4):
                 left = jnp.concatenate(
                     [half[j, i * columns:(i + 1) * columns, :] for j in range(4)], axis=1
@@ -215,9 +218,10 @@
                 mixing[slot, i * columns:(i + 1) * columns, :] = (
                     (out_scale * 2.0315) * square
                 ).astype(jnp.bfloat16)
-
-        mix(0, outer)
-        mix_copy(outer).start()
+                if send:
+                    mix_copy(i, outer).start()
+
+        mix(0, outer, True)
 
         @pl.loop(direct, chunks)
         def _(k):
@@ -226,16 +230,14 @@
             )
             row_copy(k, outer).start()
 
-        mix(1, me)
-
-        @pl.loop(0, chunks)
-        def _(k):
-            staged[rows_of(k), :] = update_rows(me, 1, rows_of(k))
-            store_copy(k).start()
-
-        @pl.loop(0, chunks)
-        def _(k):
-            store_copy(k).wait()
+        mix(1, me, False)
+
+        @pl.loop(0, chunks)
+        def _(k):
+            out_ref[rows_of(k), :] = update_rows(me, 1, rows_of(k))
+
+        @pl.loop(0, chunks)
+        def _(k):
             own_chunk(k, inner_sem.at[0, k], peer).wait_send()
             relay_chunk(outer, k, inner_sem.at[1, k], peer).wait_send()
 
@@ -245,7 +247,8 @@
             relay_chunk(peer, k, outer_sem.at[1, k], outer).wait_send()
             relay_chunk(far, k, outer_sem.at[2, k], outer).wait_send()
 
-        mix_copy(outer).wait_send()
+        for i in range(4):
+            mix_copy(i, outer).wait_send()
 
         @pl.loop(direct, chunks)
         def _(k):
@@ -267,16 +270,12 @@
             def _(k):
                 relay_chunk(shard, k, outer_sem.at[0, k], inner).wait_recv()
 
-        mix_copy(inner).wait_recv()
+        for i in range(4):
+            mix_copy(i, inner).wait_recv()
 
         @pl.loop(0, direct)
         def _(k):
-            staged[rows_of(k), :] = update_rows(me, 0, rows_of(k))
-            store_copy(k).start()
-
-        @pl.loop(0, direct)
-        def _(k):
-            store_copy(k).wait()
+            out_ref[rows_of(k), :] = update_rows(me, 0, rows_of(k))
 
         @pl.loop(0, chunks)
         def _(k):
@@ -291,41 +290,39 @@
     _, rows_all, columns = iterate.shape
     width = columns * 4
     chunks = rows_all // CHUNK
-    direct = 2 * chunks // 3 + EXTRA
+    direct = 2 * chunks // 3
     out_scale = 0.2 * math.sqrt(max(rows_all, width))
     update = pl.pallas_call(
         functools.partial(line_kernel, out_scale, chunks, direct),
-        out_shape=jax.ShapeDtypeStruct((rows_all, columns), jnp.bfloat16),
-        in_specs=[pl.BlockSpec(memory_space=pl.ANY)],
-        out_specs=pl.BlockSpec(memory_space=pl.ANY),
+        out_shape=pltpu.VMEM((rows_all, columns), jnp.bfloat16),
+        in_specs=[pl.BlockSpec(memory_space=pltpu.HBM)],
+        out_specs=pl.BlockSpec(memory_space=pltpu.VMEM),
         scratch_shapes=[
             pltpu.VMEM((4, rows_all, columns), jnp.bfloat16),
-            pltpu.VMEM((4, columns, width), jnp.float32),
+            pltpu.VMEM((4, 4, columns, columns), jnp.float32),
             pltpu.VMEM((4, width, columns), jnp.bfloat16),
             pltpu.VMEM((2, width, columns), jnp.bfloat16),
-            pltpu.VMEM((rows_all, columns), jnp.bfloat16),
             pltpu.VMEM(((chunks - direct) * CHUNK, columns), jnp.bfloat16),
             pltpu.SemaphoreType.DMA,
-            pltpu.SemaphoreType.DMA((chunks,)),
             pltpu.SemaphoreType.DMA((4, chunks)),
             pltpu.SemaphoreType.DMA((2, chunks)),
             pltpu.SemaphoreType.DMA((3, chunks)),
-            pltpu.SemaphoreType.DMA,
-            pltpu.SemaphoreType.DMA,
+            pltpu.SemaphoreType.DMA((4,)),
+            pltpu.SemaphoreType.DMA((4,)),
             pltpu.SemaphoreType.DMA((chunks,)),
             pltpu.SemaphoreType.DMA((chunks,)),
         ],
         compiler_params=pltpu.CompilerParams(
-            collective_id=0, has_side_effects=True, vmem_limit_bytes=56 << 20
+            collective_id=0, has_side_effects=True, vmem_limit_bytes=40 << 20
         ),
-    )(iterate[0])
+    )(pltpu.with_memory_space_constraint(iterate[0], pltpu.HBM))
     return update[None]
 
 
 def for_shapes(iterate):
     _, rows_all, columns = iterate.shape
     devices = lax.axis_size("fsdp")
-    fits = columns % 256 == 0 and rows_all % (3 * CHUNK * GROUP) == 0
+    fits = columns % 256 == 0 and rows_all % (3 * CHUNK) == 0
     if devices == 4 and columns * devices <= rows_all and fits:
         return on_device_line(iterate)
     return on_device(iterate)

time: 103 us -> 99.9 us (0.970)
  Pallas kernels: 101 us -> 98.6 us
  local copies, waits for them, and re-layouts: 2.65 us -> 1.15 us
    pallas_call x1, Pallas kernels: 101 us -> 98.6 us  [on_device_line(): pl.pallas_call(functools.partial(line_kernel, out_scale, chunks, direct),...]
    unnamed x1, local copies, waits for them, and re-layouts: 2.65 us -> 1.15 us
where the time goes in v1:
time: 99.9 us; the launch traced here: 99.8 us
  Pallas kernels  98.6 us (99%)
  local copies, waits for them, and re-layouts  1.15 us (1%)
    pallas_call x1, Pallas kernels, on_device_line(): pl.pallas_call(functools.partial(line_kernel, out_scale, chunks, direct),...  98.6 us

profile of v1, /device:TPU:0, one launch (start us, length us, event | category | flops | bytes accessed | tf_op | source)
XLA Modules:
  0.0 99.8 jit_solution(10563890216052949314)
XLA Ops:
  0.0 98.6 %shard_map.17 = bf16[3072,256]{1,0:T(8,128)(2,1)S(1)} custom-call(bf16[3072,256]{1,0:T(8,128)(2,1)} %bitcast.3), custom_call_target="tpu_custom_call" | custom-call | tf_op jit(solution)/shard_map/pallas_call | solution.py:295
  98.6 1.1 %copy.3 = bf16[1,3072,256]{2,1,0:T(8,128)(2,1)} copy(bf16[1,3072,256]{2,1,0:T(8,128)(2,1)S(1)} %bitcast.2) | data formatting | bytes 3145728

commit v2 on v1

--- a/solution.py
+++ b/solution.py
@@ -62,7 +62,8 @@
     return jnp.stack(results)
 
 
-CHUNK = 256
+CHUNK = 512
+FILL = 64
 SHIFT = 4.775 / (2 * 2.0315)
 BASE = 3.4445 - 4.775 * 4.775 / (4 * 2.0315)
 
@@ -71,7 +72,7 @@
     out_scale, chunks, direct,
     x_ref, out_ref,
     xall, gram, half, mixing, sent_rows,
-    local_sem, recv_sem, inner_sem, outer_sem, mix_send, mix_recv, row_send, row_recv,
+    local_sem, recv_sem, fill_send, fill_recv, inner_sem, outer_sem, mix_send, mix_recv, row_send, row_recv,
 ):
     me = lax.axis_index("fsdp")
     columns = x_ref.shape[1]
@@ -117,6 +118,23 @@
             device_id={"fsdp": target}, device_id_type=pl.DeviceIdType.MESH,
         )
 
+    fill = pl.ds(direct * CHUNK, FILL)
+    rest = pl.ds(direct * CHUNK + FILL, CHUNK - FILL)
+
+    def fill_copy(shard, source, sem, target):
+        return pltpu.make_async_remote_copy(
+            src_ref=source, dst_ref=xall.at[shard, fill],
+            send_sem=fill_send.at[sem], recv_sem=fill_recv.at[shard],
+            device_id={"fsdp": target}, device_id_type=pl.DeviceIdType.MESH,
+        )
+
+    def rest_copy(target):
+        return pltpu.make_async_remote_copy(
+            src_ref=sent_rows.at[pl.ds(FILL, CHUNK - FILL)], dst_ref=out_ref.at[rest],
+            send_sem=row_send.at[direct], recv_sem=row_recv.at[direct],
+            device_id={"fsdp": target}, device_id_type=pl.DeviceIdType.MESH,
+        )
+
     def mix_copy(i, target):
         part = pl.ds(i * columns, columns)
         return pltpu.make_async_remote_copy(
@@ -154,6 +172,8 @@
             @pl.when(k < direct)
             def _():
                 own_chunk(k, outer_sem.at[0, k], outer).start()
+
+        fill_copy(me, x_ref.at[fill], 0, outer).start()
 
         for i in range(4):
             row_ids = lax.broadcasted_iota(jnp.int32, (columns, width), 0) + i * columns
@@ -173,6 +193,10 @@
             def _():
                 relay_chunk(peer, k, outer_sem.at[1, k], outer).start()
 
+            @pl.when(k == direct)
+            def _():
+                fill_copy(peer, xall.at[peer, fill], 1, outer).start()
+
         def take_far(k):
             relay_chunk(far, k, outer_sem.at[2, k], outer).wait_recv()
 
@@ -188,6 +212,11 @@
         @pl.loop(0, chunks - 1)
         def _(k):
             take_far(k)
+
+            @pl.when(k == direct)
+            def _():
+                fill_copy(far, xall.at[far, fill], 2, outer).start()
+
             for i in range(4):
                 product = turned(xall[i, rows_of(k), :], wide(rows_of(k)))
                 for j in range(4):
@@ -223,7 +252,10 @@
 
         mix(0, outer, True)
 
-        @pl.loop(direct, chunks)
+        sent_rows[FILL:CHUNK, :] = update_rows(outer, 0, rest)
+        rest_copy(outer).start()
+
+        @pl.loop(direct + 1, chunks)
         def _(k):
             sent_rows[pl.ds(pl.multiple_of((k - direct) * CHUNK, CHUNK), CHUNK), :] = update_rows(
                 outer, 0, rows_of(k)
@@ -250,7 +282,12 @@
         for i in range(4):
             mix_copy(i, outer).wait_send()
 
-        @pl.loop(direct, chunks)
+        fill_copy(me, x_ref.at[fill], 0, outer).wait_send()
+        fill_copy(peer, xall.at[peer, fill], 1, outer).wait_send()
+        fill_copy(far, xall.at[far, fill], 2, outer).wait_send()
+        rest_copy(outer).wait_send()
+
+        @pl.loop(direct + 1, chunks)
         def _(k):
             row_copy(k, outer).wait_send()
 
@@ -270,6 +307,8 @@
             def _(k):
                 relay_chunk(shard, k, outer_sem.at[0, k], inner).wait_recv()
 
+            fill_copy(shard, xall.at[shard, fill], 0, inner).wait_recv()
+
         for i in range(4):
             mix_copy(i, inner).wait_recv()
 
@@ -277,11 +316,15 @@
         def _(k):
             out_ref[rows_of(k), :] = update_rows(me, 0, rows_of(k))
 
+        out_ref[fill, :] = update_rows(me, 0, fill)
+
         @pl.loop(0, chunks)
         def _(k):
             own_chunk(k, inner_sem.at[0, k], inner).wait_send()
 
-        @pl.loop(direct, chunks)
+        rest_copy(inner).wait_recv()
+
+        @pl.loop(direct + 1, chunks)
         def _(k):
             row_copy(k, inner).wait_recv()
 
@@ -305,6 +348,8 @@
             pltpu.VMEM(((chunks - direct) * CHUNK, columns), jnp.bfloat16),
             pltpu.SemaphoreType.DMA,
             pltpu.SemaphoreType.DMA((4, chunks)),
+            pltpu.SemaphoreType.DMA((3,)),
+            pltpu.SemaphoreType.DMA((4,)),
             pltpu.SemaphoreType.DMA((2, chunks)),
             pltpu.SemaphoreType.DMA((3, chunks)),
             pltpu.SemaphoreType.DMA((4,)),

time: 99.9 us -> 98.9 us (0.990)
  no operation moved by 1% of the time
where the time goes in v2:
time: 98.9 us; the launch traced here: 98.8 us
  Pallas kernels  97.7 us (99%)
  local copies, waits for them, and re-layouts  1.15 us (1%)
    pallas_call x1, Pallas kernels, on_device_line(): pl.pallas_call(functools.partial(line_kernel, out_scale, chunks, direct),...  97.7 us

profile of v2, /device:TPU:0, one launch (start us, length us, event | category | flops | bytes accessed | tf_op | source)
XLA Modules:
  0.0 98.8 jit_solution(15124929081155780638)
XLA Ops:
  0.0 97.7 %shard_map.17 = bf16[3072,256]{1,0:T(8,128)(2,1)S(1)} custom-call(bf16[3072,256]{1,0:T(8,128)(2,1)} %bitcast.3), custom_call_target="tpu_custom_call" | custom-call | tf_op jit(solution)/shard_map/pallas_call | solution.py:338
  97.7 1.1 %copy.3 = bf16[1,3072,256]{2,1,0:T(8,128)(2,1)} copy(bf16[1,3072,256]{2,1,0:T(8,128)(2,1)S(1)} %bitcast.2) | data formatting | bytes 3145728

commit v3 on v2

--- a/solution.py
+++ b/solution.py
@@ -327,6 +327,21 @@
         @pl.loop(direct + 1, chunks)
         def _(k):
             row_copy(k, inner).wait_recv()
+
+
+def write_out(update_ref, out_ref, sems):
+    pieces = sems.shape[0]
+    rows = out_ref.shape[0] // pieces
+    copies = [
+        pltpu.make_async_copy(
+            update_ref.at[pl.ds(i * rows, rows)], out_ref.at[pl.ds(i * rows, rows)], sems.at[i]
+        )
+        for i in range(pieces)
+    ]
+    for copy in copies:
+        copy.start()
+    for copy in copies:
+        copy.wait()
 
 
 def on_device_line(iterate):
@@ -361,7 +376,14 @@
             collective_id=0, has_side_effects=True, vmem_limit_bytes=40 << 20
         ),
     )(pltpu.with_memory_space_constraint(iterate[0], pltpu.HBM))
-    return update[None]
+    written = pl.pallas_call(
+        write_out,
+        out_shape=jax.ShapeDtypeStruct((rows_all, columns), jnp.bfloat16),
+        in_specs=[pl.BlockSpec(memory_space=pltpu.VMEM)],
+        out_specs=pl.BlockSpec(memory_space=pl.ANY),
+        scratch_shapes=[pltpu.SemaphoreType.DMA((8,))],
+    )(pltpu.with_memory_space_constraint(update, pltpu.VMEM))
+    return written[None]
 
 
 def for_shapes(iterate):

time: 98.9 us -> 99 us (level)
  Pallas kernels: 97.7 us -> 98.9 us
  local copies, waits for them, and re-layouts: 1.15 us -> 0 us
    pallas_call x0 -> x1, Pallas kernels: none -> 1.2 us  [on_device_line(): pl.pallas_call(write_out, out_shape=jax.ShapeDtypeStruct((rows_all, colum...]
    unnamed x1 -> x0, local copies, waits for them, and re-layouts: 1.15 us -> none
where the time goes in v3:
time: 99 us; the launch traced here: 98.9 us
  Pallas kernels  98.9 us (100%)
    pallas_call x1, Pallas kernels, on_device_line(): pl.pallas_call(functools.partial(line_kernel, out_scale, chunks, direct),...  97.7 us

profile of v3, /device:TPU:0, one launch (start us, length us, event | category | flops | bytes accessed | tf_op | source)
XLA Modules:
  0.0 98.9 jit_solution(12322580665992288570)
XLA Ops:
  0.0 97.7 %shard_map.17.update_ref = bf16[3072,256]{1,0:T(8,128)(2,1)S(1)} custom-call(bf16[3072,256]{1,0:T(8,128)(2,1)} %bitcast.2), custom_call_target="tpu_custom_call" | custom-call | tf_op jit(solution)/shard_map/pallas_call | solution.py:353
  97.7 1.2 %shard_map.18 = bf16[3072,256]{1,0:T(8,128)(2,1)} custom-call(bf16[3072,256]{1,0:T(8,128)(2,1)S(1)} %shard_map.17.update_ref), custom_call_target="tpu_custom_call" | custom-call | tf_op jit(solution)/shard_map/pallas_call | solution.py:379
